TPU v7x, 128 devices: a whole 4x4x4 slice. The times are simulated.
128 devices in a mesh: expert: 16 (over y, x_lo, core), tensor: 8 (over x_hi, z).
Axes of the slice: x: 4 (x_hi: 2, x_lo: 2; x = x_hi * 2 + x_lo), y: 4, z: 4, core: 2. Of those that a mesh axis runs over, the one named last changes fastest.
Arguments:
- tokens: bfloat16 [4096, 7168], P(('expert', 'tensor')), may hold values from -6 to 6
- expert_ids: int32 [4096, 2], P('expert'), may hold values from 0 to 2, all different within a row
- gate_scores: int32 [4096, 2], P('expert'), may hold values from 1 to 64
- gate_weight: bfloat16 [3, 7168, 2048], P(None, ('expert', 'tensor')), may hold values from -0.0625 to 0.0625
- up_weight: bfloat16 [3, 7168, 2048], P(None, ('expert', 'tensor')), may hold values from -0.0625 to 0.0625
- down_weight: bfloat16 [3, 7168, 2048], P(None, ('expert', 'tensor')), may hold values from -0.1875 to 0.1875
Outputs:
- mixed: bfloat16 [4096, 7168], P(('expert', 'tensor'))
Inputs may be any that keep to these rules, and one draw needn't show every extreme that they name: `expert_ids`: each row names 2 different experts.
All inputs are finite; a program needn't handle non-finite values.
Results may differ from a plain program's by a relative error of at most 0.015.
Values may be sent and summed in bfloat16 or wider, within the bound.
A program may use at most 128 MiB of HBM per device.

v0:
```python
import jax
import jax.numpy as jnp
from jax import lax
from jax.sharding import PartitionSpec as P


def activate(gate_sum, up_sum, weight_col):
    return (jax.nn.silu(gate_sum) * up_sum * weight_col).astype(jnp.bfloat16)


def local(tokens, expert_ids, gate_scores, gate_weight, up_weight, down_weight):
    gathered = lax.all_gather(tokens, "tensor", axis=0, tiled=True)
    experts = gate_weight.shape[0]
    scores = gate_scores.astype(jnp.float32)
    score_sum = jnp.sum(scores, axis=1, keepdims=True)
    labels = jnp.arange(experts, dtype=jnp.int32)
    picked = (expert_ids[:, :, None] == labels[None, None, :]).astype(jnp.float32)
    combine = jnp.sum(scores[:, :, None] * picked, axis=1) / score_sum
    served_gate, served_up, served_down = (
        lax.all_to_all(gate_weight, "tensor", split_axis=2, concat_axis=1, tiled=True),
        lax.all_to_all(up_weight, "tensor", split_axis=2, concat_axis=1, tiled=True),
        lax.all_to_all(down_weight, "tensor", split_axis=2, concat_axis=1, tiled=True),
    )
    hiddens = []
    full_gate, full_up = (
        lax.all_gather(served_gate, "expert", axis=1, tiled=True),
        lax.all_gather(served_up, "expert", axis=1, tiled=True),
    )
    for which in range(experts):
        gate_sum = jnp.dot(gathered, full_gate[which], preferred_element_type=jnp.float32)
        up_sum = jnp.dot(gathered, full_up[which], preferred_element_type=jnp.float32)
        hiddens.append(activate(gate_sum, up_sum, combine[:, which : which + 1]))
    stacked = jnp.stack(hiddens)
    partial_sum = jnp.einsum(
        "etf,edf->td",
        stacked,
        lax.all_gather(served_down, "expert", axis=1, tiled=True),
        preferred_element_type=jnp.float32,
    )
    output_rows = lax.psum_scatter(
        partial_sum.astype(jnp.bfloat16), "tensor", scatter_dimension=0, tiled=True
    )
    return output_rows


def solution(mesh):
    return jax.shard_map(
        local,
        mesh=mesh,
        in_specs=(
            P(("expert", "tensor"), None),
            P("expert", None),
            P("expert", None),
            P(None, ("expert", "tensor"), None),
            P(None, ("expert", "tensor"), None),
            P(None, ("expert", "tensor"), None),
        ),
        out_specs=P(("expert", "tensor"), None),
        check_vma=False,
    )
```

profile of v0, /device:TPU:0, one launch (start us, length us, event | category | flops | bytes accessed | tf_op | source)
XLA Modules:
  0.0 393.2 jit_solution(62899333029683740)
XLA Ops:
  6.5 0.0 all-gather.5.cloned.1.call-start
  6.5 0.7 all-gather.5.cloned.1.call-update
  7.3 0.0 all-gather.7.cloned.1.call-start
  7.3 2.8 copy.28
  10.1 2.7 reshape.8
  12.8 25.9 %all_to_all.54 = bf16[8,2,21504]{2,1,0:T(2,128)(2,1)S(1)} all-to-all(bf16[8,2,21504]{2,1,0:T(2,128)(2,1)S(1)} %reshape.8), channel_id=1, replica_groups=mesh['expert'=16,'tensor'=8] {'tensor'}, dimensions={0} | all-to-all | bytes 1376256 | tf_op jit(solution)/shard_map/all_to_all | solution.py:20
  38.8 0.0 copy-start
  38.8 3.0 reshape.9
  41.8 2.1 copy.37
  43.9 0.0 all-gather.7.cloned.1.call-update
  44.0 0.0 all-gather.9.cloned.1.call-start
  44.0 0.0 copy-done
  44.0 1.4 copy.31
  45.4 2.7 reshape.6
  48.1 20.4 %all_to_all.55 = bf16[8,2,21504]{2,1,0:T(2,128)(2,1)S(1)} all-to-all(bf16[8,2,21504]{2,1,0:T(2,128)(2,1)S(1)} %reshape.6), channel_id=1, replica_groups=mesh['expert'=16,'tensor'=8] {'tensor'}, dimensions={0} | all-to-all | bytes 1376256 | tf_op jit(solution)/shard_map/all_to_all | solution.py:21
  68.5 0.0 copy-start.1
  68.5 3.0 reshape.7
  71.5 2.2 copy.39
  73.7 0.0 all-gather.9.cloned.1.call-update
  73.7 0.0 all-gather.11.cloned.1.call-start
  73.8 0.0 copy-done.1
  73.8 1.4 copy.34
  75.1 2.7 reshape.4
  77.8 0.0 copy-start.2
  77.9 0.0 copy-start.3
  77.9 14.4 %all_to_all.56 = bf16[8,2,21504]{2,1,0:T(2,128)(2,1)S(1)} all-to-all(bf16[8,2,21504]{2,1,0:T(2,128)(2,1)S(1)} %reshape.4), channel_id=1, replica_groups=mesh['expert'=16,'tensor'=8] {'tensor'}, dimensions={0} | all-to-all | bytes 1376256 | tf_op jit(solution)/shard_map/all_to_all | solution.py:22
  92.2 3.0 reshape.5
  95.2 2.2 copy.35
  97.4 0.0 all-gather.11.cloned.1.call-update
  97.4 0.2 reduce-scatter.2.cloned.1.call-start
  97.6 0.0 copy-done.2
  97.7 0.0 copy-done.3
  97.7 0.0 all-gather.5.cloned.1.call-done
  97.8 58.9 %all-gather.7.cloned.1.call-done = bf16[3,7168,256]{2,1,0:T(8,128)(2,1)} async-done(((bf16[3,448,256]{2,1,0:T(8,128)(2,1)}), bf16[3,7168,256]{2,1,0:T(8,128)(2,1)}) %all-gather.7.cloned.1.call-update) | async-done | bytes 11010064 | tf_op jit(solution)/shard_map/all_gather | solution.py:26
  156.7 0.0 copy-start.4
  156.7 4.4 %fusion.2 = f32[256,256]{1,0:T(8,128)S(1)} fusion(bf16[256,7168]{1,0:T(8,128)(2,1)} %all-gather.5.cloned.1.call-done, bf16[3,7168,256]{2,1,0:T(8,128)(2,1)} %all-gather.7.cloned.1.call-done), kind=kOutput, calls=%fused_computation.5 | convolution fusion | flops 939524096 | bytes 7602176 | tf_op jit(solution)/shard_map/dot_general | solution.py:30
  161.1 0.0 copy-done.4
  161.1 3.2 fusion.4
  164.3 3.2 fusion.6
  167.6 56.2 %all-gather.9.cloned.1.call-done = bf16[3,7168,256]{2,1,0:T(8,128)(2,1)} async-done(((bf16[3,448,256]{2,1,0:T(8,128)(2,1)}), bf16[3,7168,256]{2,1,0:T(8,128)(2,1)}) %all-gather.9.cloned.1.call-update) | async-done | bytes 11010064 | tf_op jit(solution)/shard_map/all_gather | solution.py:27
  223.8 4.4 %fusion.18 = bf16[1,256,256]{2,1,0:T(8,128)(2,1)S(1)} fusion(bf16[256,7168]{1,0:T(8,128)(2,1)} %all-gather.5.cloned.1.call-done, bf16[3,7168,256]{2,1,0:T(8,128)(2,1)} %all-gather.9.cloned.1.call-done, f32[256,256]{1,0:T(8,128)S(1)} %fusion.2, f32[256]{0:T(256)S(1)} %bitcast.93), kind=kOutput, calls=%fused_computation.25 | convolution fusion | flops 939982848 | bytes 7734272 | tf_op jit(solution)/shard_map/dot_general | solution.py:31
  228.2 0.0 copy-done.5
  228.2 3.2 fusion.17
  231.4 3.2 fusion.16
  234.6 56.2 %all-gather.11.cloned.1.call-done = bf16[3,7168,256]{2,1,0:T(8,128)(2,1)} async-done(((bf16[3,448,256]{2,1,0:T(8,128)(2,1)}), bf16[3,7168,256]{2,1,0:T(8,128)(2,1)}) %all-gather.11.cloned.1.call-update) | async-done | bytes 11010064 | tf_op jit(solution)/shard_map/all_gather | solution.py:37
  290.8 12.7 %fusion = bf16[256,7168]{1,0:T(8,128)(2,1)} fusion(bf16[3,7168,256]{2,1,0:T(8,128)(2,1)} %all-gather.11.cloned.1.call-done, bf16[1,256,256]{2,1,0:T(8,128)(2,1)S(1)} %fusion.18, bf16[1,256,256]{2,1,0:T(8,128)(2,1)S(1)} %fusion.17, bf16[1,256,256]{2,1,0:T(8,128)(2,1)S(1)} %fusion.16), kind=kOutput, calls=%fused_computation.1 | convolution fusion | flops 2820800512 | bytes 15073280 | tf_op jit(solution)/shard_map/etf,edf->td/dot_general | solution.py:34
  303.4 0.0 reduce-scatter.2.cloned.1.call-update
  303.5 83.2 %reduce-scatter.2.cloned.1.call-done = bf16[32,7168]{1,0:T(8,128)(2,1)} async-done(((bf16[256,7168]{1,0:T(8,128)(2,1)}), bf16[32,7168]{1,0:T(8,128)(2,1)}) %reduce-scatter.2.cloned.1.call-update) | async-done | bytes 458768 | tf_op jit(solution)/shard_map/reduce_scatter | solution.py:40
  (6 shorter events, 0.1 us)
Async XLA Ops:
  6.5 91.2 %all-gather.5.cloned.1.call-start = ((), (), s32[]{:S(2)}) async-start(), calls=%async_computation.4 | async-start | bytes 4128768 | tf_op jit(solution)/shard_map/all_gather | solution.py:12
  7.3 149.4 %all-gather.7.cloned.1.call-start = ((), (), s32[]{:S(2)}) async-start(), calls=%async_computation.5 | async-start | bytes 11698176 | tf_op jit(solution)/shard_map/all_gather | solution.py:26
  38.8 5.2 %copy-start = (bf16[3,56,2048]{2,1,0:T(8,128)(2,1)S(1)}, bf16[3,56,2048]{2,1,0:T(8,128)(2,1)}, u32[]{:S(2)}) copy-start(bf16[3,56,2048]{2,1,0:T(8,128)(2,1)} %param.10) | copy-start | bytes 2064388
  44.0 179.8 %all-gather.9.cloned.1.call-start = ((), (), s32[]{:S(2)}) async-start(), calls=%async_computation.6 | async-start | bytes 11698176 | tf_op jit(solution)/shard_map/all_gather | solution.py:27
  68.5 5.3 %copy-start.1 = (bf16[3,56,2048]{2,1,0:T(8,128)(2,1)S(1)}, bf16[3,56,2048]{2,1,0:T(8,128)(2,1)}, u32[]{:S(2)}) copy-start(bf16[3,56,2048]{2,1,0:T(8,128)(2,1)} %param.11) | copy-start | bytes 2064388
  73.7 217.1 %all-gather.11.cloned.1.call-start = ((), (), s32[]{:S(2)}) async-start(), calls=%async_computation.7 | async-start | bytes 11698176 | tf_op jit(solution)/shard_map/all_gather | solution.py:37
  77.8 19.8 %copy-start.2 = (s32[256,2]{0,1:T(2,128)S(1)}, s32[256,2]{0,1:T(2,128)}, u32[]{:S(2)}) copy-start(s32[256,2]{0,1:T(2,128)} %param.8) | copy-start | bytes 6148
  77.9 19.8 %copy-start.3 = (s32[256,2]{0,1:T(2,128)S(1)}, s32[256,2]{0,1:T(2,128)}, u32[]{:S(2)}) copy-start(s32[256,2]{0,1:T(2,128)} %param.7) | copy-start | bytes 6148
  97.4 289.3 %reduce-scatter.2.cloned.1.call-start = ((), (), s32[]{:S(2)}) async-start(), calls=%async_computation.8 | async-start | bytes 4128768 | tf_op jit(solution)/shard_map/reduce_scatter | solution.py:40
  156.7 4.4 %copy-start.4 = (bf16[256,7168]{1,0:T(8,128)(2,1)S(1)}, bf16[256,7168]{1,0:T(8,128)(2,1)}, u32[]{:S(2)}) copy-start(bf16[256,7168]{1,0:T(8,128)(2,1)} %all-gather.5.cloned.1.call-done) | copy-start | bytes 11010052
  223.8 4.4 %copy-start.5 = (bf16[256,7168]{1,0:T(8,128)(2,1)S(1)}, bf16[256,7168]{1,0:T(8,128)(2,1)}, u32[]{:S(2)}) copy-start(bf16[256,7168]{1,0:T(8,128)(2,1)} %all-gather.5.cloned.1.call-done) | copy-start | bytes 11010052
Sparse Core Ops, SparseCore 0:
  9.7 83.9 all-gather.4
  95.3 61.3 all-gather.6
  158.4 65.3 all-gather.8
  225.3 65.3 all-gather.10
  303.6 83.0 reduce-scatter.1
where the time goes:
time: 394 us; the launch traced here: 393 us
  waiting for transfers between devices  255 us (65%)
  blocking collectives  60.7 us (15%)
  matrix products  34.3 us (9%)
  local copies, waits for them, and re-layouts  29.2 us (7%)
  between operations  13.3 us (3%)
    reduce_scatter x1, waiting for transfers between devices, local(): lax.psum_scatter(partial_sum.astype(jnp.bfloat16), 'tensor', scatter_dime...  83.2 us
    all_gather x1, waiting for transfers between devices, local(): lax.all_gather(served_gate, 'expert', axis=1, tiled=True)  58.9 us
    all_gather x1, waiting for transfers between devices, local(): lax.all_gather(served_up, 'expert', axis=1, tiled=True)  56.2 us
    all_gather x1, waiting for transfers between devices, local(): lax.all_gather(served_down, 'expert', axis=1, tiled=True)  56.2 us
    all_to_all x1, blocking collectives, local(): lax.all_to_all(gate_weight, 'tensor', split_axis=2, concat_axis=1, tiled=...  25.9 us
    unnamed x21, local copies, waits for them, and re-layouts  22.7 us
    all_to_all x1, blocking collectives, local(): lax.all_to_all(up_weight, 'tensor', split_axis=2, concat_axis=1, tiled=True)  20.4 us
    all_to_all x1, blocking collectives, local(): lax.all_to_all(down_weight, 'tensor', split_axis=2, concat_axis=1, tiled=...  14.4 us
  transfers between devices with their start and end apart: 5, of which 4 were waited for; matrix products, arithmetic and copies ran while one was open for 13% of the time, Pallas kernels for 0%

commit v1 on v0

--- a/solution.py
+++ b/solution.py
@@ -24,7 +24,9 @@
     hiddens = []
     full_gate, full_up = (
         lax.all_gather(served_gate, "expert", axis=1, tiled=True),
-        lax.all_gather(served_up, "expert", axis=1, tiled=True),
+        jnp.concatenate(
+            lax.all_to_all(jnp.stack([served_up] * lax.axis_size("expert")), "expert", 0, 0), axis=1
+        ),
     )
     for which in range(experts):
         gate_sum = jnp.dot(gathered, full_gate[which], preferred_element_type=jnp.float32)

time: 394 us -> 459 us (1.16)
  waiting for transfers between devices: 255 us -> 308 us
  local copies, waits for them, and re-layouts: 29.2 us -> 45 us
  matrix products: 34.3 us -> 25.7 us
  starting transfers between devices: 0.35 us -> 5.7 us
    all_to_all x0 -> x1, waiting for transfers between devices: none -> 189 us  [local(): lax.all_to_all(jnp.stack([served_up] * lax.axis_size('expert')), 'expert'...]
    all_gather x1, waiting for transfers between devices: 58.9 us -> 0.01 us  [local(): lax.all_gather(served_gate, 'expert', axis=1, tiled=True)]
    all_gather x1 -> x0, waiting for transfers between devices: 56.2 us -> none  [local(): lax.all_gather(served_up, 'expert', axis=1, tiled=True)]
    all_gather x1, waiting for transfers between devices: 56.2 us -> 35 us  [local(): lax.all_gather(served_down, 'expert', axis=1, tiled=True)]
    slice x0 -> x1, local copies, waits for them, and re-layouts: none -> 7.94 us  [local(): full_up[which]]
    all_to_all x1, blocking collectives: 14.4 us -> 20.4 us  [local(): lax.all_to_all(down_weight, 'tensor', split_axis=2, concat_axis=1, tiled=...]
    all_to_all x1, blocking collectives: 20.4 us -> 14.3 us  [local(): lax.all_to_all(up_weight, 'tensor', split_axis=2, concat_axis=1, tiled=True)]
    another operation x0 -> x1, local copies, waits for them, and re-layouts: none -> 5.43 us  [local(): jnp.stack([served_up] * lax.axis_size('expert'))]
  transfers between devices with their start and end apart: 5 -> 5, of which waited for: 4 -> 3; matrix products, arithmetic and copies ran while one was open for 13% -> 12% of each run, Pallas kernels for 0% -> 0%
where the time goes in v1:
time: 459 us
  waiting for transfers between devices  308 us (67%)
  blocking collectives  60.7 us (13%)
  local copies, waits for them, and re-layouts  45 us (10%)
  matrix products  25.7 us (6%)
  between operations  13.4 us (3%)
  starting transfers between devices  5.7 us (1%)
    all_to_all x1, waiting for transfers between devices, local(): lax.all_to_all(jnp.stack([served_up] * lax.axis_size('expert')), 'expert'...  189 us
    reduce_scatter x1, waiting for transfers between devices, local(): lax.psum_scatter(partial_sum.astype(jnp.bfloat16), 'tensor', scatter_dime...  83.5 us
    all_gather x1, waiting for transfers between devices, local(): lax.all_gather(served_down, 'expert', axis=1, tiled=True)  35 us
    unnamed x27, local copies, waits for them, and re-layouts  26.2 us
    all_to_all x1, blocking collectives, local(): lax.all_to_all(gate_weight, 'tensor', split_axis=2, concat_axis=1, tiled=...  25.9 us
    all_to_all x1, blocking collectives, local(): lax.all_to_all(down_weight, 'tensor', split_axis=2, concat_axis=1, tiled=...  20.4 us
    all_to_all x1, blocking collectives, local(): lax.all_to_all(up_weight, 'tensor', split_axis=2, concat_axis=1, tiled=True)  14.3 us
    dot_general x1, matrix products, local(): jnp.einsum('etf,edf->td', stacked, lax.all_gather(served_down, 'expert',...  12.5 us
  transfers between devices with their start and end apart: 5, of which 3 were waited for; matrix products, arithmetic and copies ran while one was open for 12% of the time, Pallas kernels for 0%

profile of v1, /device:TPU:0, one launch (start us, length us, event | category | flops | bytes accessed | tf_op | source)
XLA Modules:
  0.0 458.5 jit_solution(9005072131616238800)
XLA Ops:
  6.5 0.0 all-gather.4.cloned.1.call-start
  6.5 0.7 all-gather.4.cloned.1.call-update
  7.3 0.0 all-gather.6.cloned.1.call-start
  7.3 2.8 copy.28
  10.1 2.7 reshape.22
  12.8 25.9 %all_to_all.56 = bf16[8,2,21504]{2,1,0:T(2,128)(2,1)S(1)} all-to-all(bf16[8,2,21504]{2,1,0:T(2,128)(2,1)S(1)} %reshape.22), channel_id=1, replica_groups=mesh['expert'=16,'tensor'=8] {'tensor'}, dimensions={0} | all-to-all | bytes 1376256 | tf_op jit(solution)/shard_map/all_to_all | solution.py:20
  38.8 3.0 reshape.23
  41.8 2.2 copy.37
  44.0 0.0 all-gather.6.cloned.1.call-update
  44.0 0.0 all-gather.8.cloned.1.call-start
  44.0 0.0 copy-done.3
  44.0 1.4 copy.34
  45.4 2.7 reshape.18
  48.1 20.4 %all_to_all.57 = bf16[8,2,21504]{2,1,0:T(2,128)(2,1)S(1)} all-to-all(bf16[8,2,21504]{2,1,0:T(2,128)(2,1)S(1)} %reshape.18), channel_id=1, replica_groups=mesh['expert'=16,'tensor'=8] {'tensor'}, dimensions={0} | all-to-all | bytes 1376256 | tf_op jit(solution)/shard_map/all_to_all | solution.py:22
  68.5 3.0 reshape.19
  71.5 2.2 copy.35
  73.7 0.0 all-gather.8.cloned.1.call-update
  73.7 0.0 copy-done.4
  73.8 1.4 copy.31
  75.1 2.7 reshape.20
  77.8 14.3 %all_to_all.58 = bf16[8,2,21504]{2,1,0:T(2,128)(2,1)S(1)} all-to-all(bf16[8,2,21504]{2,1,0:T(2,128)(2,1)S(1)} %reshape.20), channel_id=1, replica_groups=mesh['expert'=16,'tensor'=8] {'tensor'}, dimensions={0} | all-to-all | bytes 1376256 | tf_op jit(solution)/shard_map/all_to_all | solution.py:21
  92.2 3.0 reshape.21
  95.2 1.1 copy.39
  96.3 5.4 %stack.13 = bf16[16,3,448,256]{3,2,1,0:T(8,128)(2,1)} broadcast(bf16[3,448,256]{2,1,0:T(8,128)(2,1)S(1)} %bitcast.67), dimensions={1,2,3} | broadcast | bytes 11698176 | tf_op jit(solution)/shard_map/stack | solution.py:28
  101.7 5.4 %all-to-all-start.2 = ((bf16[16,3,448,256]{3,2,1,0:T(8,128)(2,1)}), bf16[16,3,448,256]{3,2,1,0:T(8,128)(2,1)}, u32[]{:S(2)}, u32[]{:S(2)}) async-start(bf16[16,3,448,256]{3,2,1,0:T(8,128)(2,1)} %stack.13), calls=%async_computation.2 | async-start | bytes 22020096 | tf_op jit(solution)/shard_map/all_to_all | solution.py:28
  107.1 0.2 reduce-scatter.2.cloned.1.call-start
  107.4 0.0 copy-done.5
  107.4 0.0 copy-done.6
  107.4 188.8 %all-to-all-done.2 = bf16[16,3,448,256]{3,2,1,0:T(8,128)(2,1)} async-done(((bf16[16,3,448,256]{3,2,1,0:T(8,128)(2,1)}), bf16[16,3,448,256]{3,2,1,0:T(8,128)(2,1)}, u32[]{:S(2)}, u32[]{:S(2)}) %all-to-all-start.2) | async-done | bytes 11010080 | tf_op jit(solution)/shard_map/all_to_all | solution.py:28
  296.2 7.9 %fusion.20 = (bf16[1,16,448,256]{3,2,0,1:T(8,128)(2,1)}, bf16[1,16,448,256]{3,2,0,1:T(8,128)(2,1)}, bf16[1,16,448,256]{3,2,0,1:T(8,128)(2,1)}) fusion(bf16[3,16,448,256]{3,2,0,1:T(8,128)(2,1)} %bitcast.9), kind=kLoop, calls=%fused_computation.30 | loop fusion | bytes 22020096 | tf_op jit(solution)/shard_map/slice | solution.py:33
  304.2 0.0 copy-start.7
  304.2 4.5 fusion.1
  308.7 0.0 copy-done.2
  308.7 0.0 copy-start.8
  308.7 4.2 fusion.10
  312.9 0.2 copy-done.7
  313.1 1.4 copy-done.8
  314.5 1.1 fusion.2
  315.6 1.0 copy-done.1
  316.6 1.1 fusion.11
  317.7 0.0 copy-start
  317.7 1.1 fusion.3
  318.8 1.0 copy-done
  319.8 1.1 fusion.12
  321.0 35.0 %all-gather.8.cloned.1.call-done = bf16[3,7168,256]{2,1,0:T(8,128)(2,1)} async-done(((bf16[3,448,256]{2,1,0:T(8,128)(2,1)}), bf16[3,7168,256]{2,1,0:T(8,128)(2,1)}) %all-gather.8.cloned.1.call-update) | async-done | bytes 11010064 | tf_op jit(solution)/shard_map/all_gather | solution.py:39
  356.0 12.5 %fusion = bf16[256,7168]{1,0:T(8,128)(2,1)} fusion(bf16[3,7168,256]{2,1,0:T(8,128)(2,1)} %all-gather.8.cloned.1.call-done, bf16[1,256,256]{2,1,0:T(8,128)(2,1)S(1)} %fusion.10, bf16[1,256,256]{2,1,0:T(8,128)(2,1)S(1)} %fusion.11, bf16[1,256,256]{2,1,0:T(8,128)(2,1)S(1)} %fusion.12), kind=kOutput, calls=%fused_computation.1 | convolution fusion | flops 2820800512 | bytes 15073280 | tf_op jit(solution)/shard_map/etf,edf->td/dot_general | solution.py:36
  368.5 0.0 reduce-scatter.2.cloned.1.call-update
  368.5 83.5 %reduce-scatter.2.cloned.1.call-done = bf16[32,7168]{1,0:T(8,128)(2,1)} async-done(((bf16[256,7168]{1,0:T(8,128)(2,1)}), bf16[32,7168]{1,0:T(8,128)(2,1)}) %reduce-scatter.2.cloned.1.call-update) | async-done | bytes 458768 | tf_op jit(solution)/shard_map/reduce_scatter | solution.py:42
  (13 shorter events, 0.1 us)
Async XLA Ops:
  6.5 297.6 %all-gather.4.cloned.1.call-start = ((), (), s32[]{:S(2)}) async-start(), calls=%async_computation.5 | async-start | bytes 4128768 | tf_op jit(solution)/shard_map/all_gather | solution.py:12
  7.3 296.9 %all-gather.6.cloned.1.call-start = ((), (), s32[]{:S(2)}) async-start(), calls=%async_computation.6 | async-start | bytes 11698176 | tf_op jit(solution)/shard_map/all_gather | solution.py:26
  38.8 5.3 %copy-start.3 = (bf16[3,56,2048]{2,1,0:T(8,128)(2,1)S(1)}, bf16[3,56,2048]{2,1,0:T(8,128)(2,1)}, u32[]{:S(2)}) copy-start(bf16[3,56,2048]{2,1,0:T(8,128)(2,1)} %param.11) | copy-start | bytes 2064388
  44.0 312.0 %all-gather.8.cloned.1.call-start = ((), (), s32[]{:S(2)}) async-start(), calls=%async_computation.7 | async-start | bytes 11698176 | tf_op jit(solution)/shard_map/all_gather | solution.py:39
  68.5 5.2 %copy-start.4 = (bf16[3,56,2048]{2,1,0:T(8,128)(2,1)S(1)}, bf16[3,56,2048]{2,1,0:T(8,128)(2,1)}, u32[]{:S(2)}) copy-start(bf16[3,56,2048]{2,1,0:T(8,128)(2,1)} %param.10) | copy-start | bytes 2064388
  101.7 5.6 %copy-start.5 = (s32[256,2]{0,1:T(2,128)S(1)}, s32[256,2]{0,1:T(2,128)}, u32[]{:S(2)}) copy-start(s32[256,2]{0,1:T(2,128)} %param.8) | copy-start | bytes 6148
  101.7 5.7 %copy-start.6 = (s32[256,2]{0,1:T(2,128)S(1)}, s32[256,2]{0,1:T(2,128)}, u32[]{:S(2)}) copy-start(s32[256,2]{0,1:T(2,128)} %param.7) | copy-start | bytes 6148
  101.7 194.5 %all-to-all-start.2 = ((bf16[16,3,448,256]{3,2,1,0:T(8,128)(2,1)}), bf16[16,3,448,256]{3,2,1,0:T(8,128)(2,1)}, u32[]{:S(2)}, u32[]{:S(2)}) async-start(bf16[16,3,448,256]{3,2,1,0:T(8,128)(2,1)} %stack.13), calls=%async_computation.2 | async-start | bytes 22020096 | tf_op jit(solution)/shard_map/all_to_all | solution.py:28
  107.1 344.9 %reduce-scatter.2.cloned.1.call-start = ((), (), s32[]{:S(2)}) async-start(), calls=%async_computation.8 | async-start | bytes 4128768 | tf_op jit(solution)/shard_map/reduce_scatter | solution.py:42
  304.2 4.5 copy-start.2
  304.2 9.0 %copy-start.7 = (bf16[3,7168,256]{2,1,0:T(8,128)(2,1)S(1)}, bf16[3,7168,256]{2,1,0:T(8,128)(2,1)}, u32[]{:S(2)}) copy-start(bf16[3,7168,256]{2,1,0:T(8,128)(2,1)} %all-gather.6.cloned.1.call-done) | copy-start | bytes 33030148
  308.7 5.8 %copy-start.8 = (bf16[256,7168]{1,0:T(8,128)(2,1)S(1)}, bf16[256,7168]{1,0:T(8,128)(2,1)}, u32[]{:S(2)}) copy-start(bf16[256,7168]{1,0:T(8,128)(2,1)} %all-gather.4.cloned.1.call-done) | copy-start | bytes 11010052
  314.5 2.1 copy-start.1
  317.7 2.2 copy-start
Sparse Core Ops, SparseCore 0:
  9.7 83.9 all-gather.3
  95.3 185.5 all-gather.5
  282.6 73.3 all-gather.7
  368.6 83.3 reduce-scatter.1
